TPU v7x, 32 devices: a whole 2x2x4 slice. The times are simulated.
32 devices in a mesh: seq: 8 (over y, x, core), ch: 4 (over z).
Axes of the slice: x: 2, y: 2, z: 4, core: 2. Of those that a mesh axis runs over, the one named last changes fastest.
Arguments:
- inputs: bfloat16 [1536, 131072], P('ch', 'seq'), may hold values from -6 to 6
- gating: bfloat16 [1536, 131072], P('ch', 'seq'), may hold values from -6 to 6
- upstream: bfloat16 [1536, 131072], P('ch', 'seq'), may hold values from -6 to 6
- factor_one: bfloat16 [512, 512], replicated, may hold values from -0.25 to 0.25
- factor_two: bfloat16 [256, 256], replicated, may hold values from -0.375 to 0.375
- factor_three: bfloat16 [256, 256], replicated, may hold values from -0.375 to 0.375
- factor_four: bfloat16 [512, 512], replicated, may hold values from -0.25 to 0.25
- kernel_cols: float32 [1536, 512], P('ch'), may hold values from -4 to 4
- kernel_rows: float32 [1536, 256], P('ch'), may hold values from -4 to 4
Outputs:
- input_grad: bfloat16 [1536, 131072], P('ch', 'seq')
- gating_grad: bfloat16 [1536, 131072], P('ch', 'seq')
- one_grad: float32 [512, 512], replicated
- two_grad: float32 [256, 256], replicated
- three_grad: float32 [256, 256], replicated
- four_grad: float32 [512, 512], replicated
- cols_grad: float32 [1536, 512], P('ch')
- rows_grad: float32 [1536, 256], P('ch')
All inputs are finite; a program needn't handle non-finite values.
Results may differ from a plain program's by a relative error of at most 0.0076.
Values may be sent and summed in bfloat16 or wider, within the bound.
A program may use at most 384 MiB of HBM per device.

v0:
```python
import math
import jax
import jax.numpy as jnp
from jax import lax
from jax.sharding import PartitionSpec as P

P1 = 256
P2 = 512
C = 1536


def local(
    inputs,
    gating,
    upstream,
    factor_one,
    factor_two,
    factor_three,
    factor_four,
    kernel_cols,
    kernel_rows,
):
    width = inputs.shape[0]
    length = inputs.shape[1]
    parts = lax.axis_size("seq")
    flt = jnp.float32
    half = jnp.bfloat16
    rows_local = length // P2
    up_gate = (upstream.astype(flt) * gating.astype(flt)).astype(half)
    moved_in, moved_gate = (
        lax.all_to_all(inputs, "seq", split_axis=0, concat_axis=1, tiled=True),
        lax.all_to_all(up_gate, "seq", split_axis=0, concat_axis=1, tiled=True),
    )
    several = width // parts
    offset = lax.axis_index("seq") * several
    local_cols = lax.dynamic_slice_in_dim(kernel_cols, offset, several, 0)
    local_rows = lax.dynamic_slice_in_dim(kernel_rows, offset, several, 0)
    shaped = moved_in.reshape(several, P1, P2)
    gate_rows = moved_gate.reshape(several, P1, P2)
    first_prod = jnp.einsum("cij,jk->cik", shaped, factor_one, preferred_element_type=flt)
    first_out = (first_prod * local_cols[:, None, :]).astype(half)
    left_prod = jnp.einsum("ki,cij->ckj", factor_two, first_out, preferred_element_type=flt)
    left_out = (left_prod * local_rows[:, :, None]).astype(half)
    second = jnp.einsum("ki,cij->ckj", factor_three, left_out, preferred_element_type=flt).astype(
        half
    )
    grad_four = jnp.einsum("cij,cik->jk", second, gate_rows, preferred_element_type=flt)
    grad_second = jnp.einsum(
        "cik,jk->cij", gate_rows, factor_four, preferred_element_type=flt
    ).astype(half)
    grad_three = jnp.einsum("ckj,cij->ki", grad_second, left_out, preferred_element_type=flt)
    grad_left = jnp.einsum("ki,ckj->cij", factor_three, grad_second, preferred_element_type=flt)
    rows_part = jnp.sum(grad_left * left_prod, axis=2)
    grad_prod = (grad_left * local_rows[:, :, None]).astype(half)
    grad_two = jnp.einsum("ckj,cij->ki", grad_prod, first_out, preferred_element_type=flt)
    grad_first = jnp.einsum(
        "ki,ckj->cij", factor_two, grad_prod, preferred_element_type=flt
    ).astype(half)
    cols_part = jnp.sum(grad_first.astype(flt) * first_prod, axis=1)
    grad_inner = (grad_first.astype(flt) * local_cols[:, None, :]).astype(half)
    grad_one = jnp.einsum("cij,cik->jk", shaped, grad_inner, preferred_element_type=flt)
    local_input = jnp.einsum(
        "cik,jk->cij", grad_inner, factor_one, preferred_element_type=flt
    ).astype(half)
    input_grad, second_rows = (
        lax.all_to_all(
            local_input.reshape(several, P1 * P2), "seq", split_axis=1, concat_axis=0, tiled=True
        ),
        lax.all_to_all(
            second.reshape(several, P1 * P2), "seq", split_axis=1, concat_axis=0, tiled=True
        ),
    )
    cols_sum, rows_sum = (
        lax.all_gather(cols_part, "seq", axis=0, tiled=True),
        lax.all_gather(rows_part, "seq", axis=0, tiled=True),
    )
    final_prod = jnp.einsum(
        "cij,jk->cik",
        second_rows.reshape(width, rows_local, P2),
        factor_four,
        preferred_element_type=flt,
    )
    gating_grad = (
        (upstream.reshape(width, rows_local, P2).astype(flt) * final_prod)
        .astype(half)
        .reshape(width, length)
    )
    one_sum, two_sum, three_sum, four_sum = lax.psum(
        (grad_one, grad_two, grad_three, grad_four), ("seq", "ch")
    )
    scale_one = 1.0 / math.sqrt(P1 * C)
    scale_two = 1.0 / math.sqrt(P2 * C)
    return (
        input_grad,
        gating_grad,
        one_sum * scale_one,
        two_sum * scale_two,
        three_sum * scale_two,
        four_sum * scale_one,
        cols_sum / math.sqrt(P1),
        rows_sum / math.sqrt(P2),
    )


def solution(mesh):
    in_specs = (
        P("ch", "seq"),
        P("ch", "seq"),
        P("ch", "seq"),
        P(),
        P(),
        P(),
        P(),
        P("ch", None),
        P("ch", None),
    )
    out_specs = (P("ch", "seq"), P("ch", "seq"), P(), P(), P(), P(), P("ch", None), P("ch", None))
    return jax.shard_map(local, mesh=mesh, in_specs=in_specs, out_specs=out_specs, check_vma=False)
```

profile of v0, /device:TPU:0, one launch (start us, length us, event | category | flops | bytes accessed | tf_op | source)
XLA Modules:
  0.0 879.9 jit_solution(3477879930901490185)
XLA Ops:
  17.1 144.0 %all_to_all.67 = bf16[8,48,16384]{2,1,0:T(8,128)(2,1)} all-to-all(bf16[8,48,16384]{2,1,0:T(8,128)(2,1)S(1)} %bitcast.84), channel_id=1, replica_groups=mesh['seq'=8,'ch'=4] {'seq'}, dimensions={0} | all-to-all | bytes 25165824 | tf_op jit(solution)/shard_map/all_to_all | solution.py:32
  167.3 14.4 %copy.71 = bf16[48,8,16384]{2,1,0:T(8,128)(2,1)} copy(bf16[48,8,16384]{2,0,1:T(8,128)(2,1)} %bitcast.82) | data formatting | bytes 25165824 | tf_op jit(solution)/shard_map/all_to_all | solution.py:32
  181.7 19.5 %reshape.52 = bf16[48,256,512]{2,1,0:T(8,128)(2,1)} reshape(bf16[48,8,16384]{2,1,0:T(8,128)(2,1)} %copy.71) | data formatting | bytes 25165824 | tf_op jit(solution)/shard_map/reshape | solution.py:39
  201.3 11.6 %convolution_convert_fusion.1 = bf16[48,256,512]{2,1,0:T(8,128)(2,1)S(1)} fusion(bf16[48,256,512]{2,1,0:T(8,128)(2,1)} %reshape.52, bf16[512,512]{1,0:T(8,128)(2,1)S(1)} %copy-done.4), kind=kOutput, calls=%fused_computation.19 | convolution fusion | flops 6448742400 | bytes 25690112 | tf_op jit(solution)/shard_map/cik,jk->cij/dot_general | solution.py:48
  217.4 10.1 %fusion.39 = f32[48,512,256]{2,1,0:T(8,128)} fusion(bf16[48,256,512]{2,1,0:T(8,128)(2,1)S(1)} %convolution_convert_fusion.1, bf16[256,256]{1,0:T(8,128)(2,1)S(1)} %copy-done.7), kind=kOutput, calls=%fused_computation.39 | convolution fusion | flops 3221225472 | bytes 37879808 | tf_op jit(solution)/shard_map/ki,ckj->cij/dot_general | solution.py:52
  227.5 14.8 %convolution_convert_fusion = bf16[48,512,256]{1,2,0:T(8,128)(2,1)} fusion(f32[48,512,256]{2,1,0:T(8,128)} %fusion.39, f32[48,256]{1,0:T(8,128)S(1)} %constant_dynamic-slice_fusion.1, bf16[256,256]{1,0:T(8,128)(2,1)S(1)} %copy-done.6), kind=kOutput, calls=%fused_computation.17 | convolution fusion | flops 3240099840 | bytes 37928960 | tf_op jit(solution)/shard_map/ki,ckj->cij/dot_general | solution.py:56
  242.3 14.4 %fusion.10 = bf16[48,256,512]{2,1,0:T(8,128)(2,1)} fusion(bf16[48,512,256]{1,2,0:T(8,128)(2,1)} %convolution_convert_fusion, f32[48,512]{1,0:T(8,128)S(1)} %constant_dynamic-slice_fusion, bf16[512,512]{1,0:T(8,128)(2,1)S(1)} %copy-done.3), kind=kOutput, calls=%fused_computation.18 | convolution fusion | flops 6467616768 | bytes 25788416 | tf_op jit(solution)/shard_map/cik,jk->cij/dot_general | solution.py:62
  256.7 19.8 %all_to_all.53 = bf16[48,8,16384]{2,1,0:T(8,128)(2,1)} reshape(bf16[48,256,512]{2,1,0:T(8,128)(2,1)} %fusion.10) | data formatting | bytes 25165824 | tf_op jit(solution)/shard_map/all_to_all | solution.py:66
  276.5 14.5 %copy.75 = bf16[48,8,16384]{2,0,1:T(8,128)(2,1)} copy(bf16[48,8,16384]{2,1,0:T(8,128)(2,1)} %all_to_all.53) | data formatting | bytes 25165824 | tf_op jit(solution)/shard_map/all_to_all | solution.py:66
  291.0 14.5 %all-to-all-done.2 = bf16[8,48,16384]{2,1,0:T(8,128)(2,1)} async-done(((bf16[8,48,16384]{2,1,0:T(8,128)(2,1)}), bf16[8,48,16384]{2,1,0:T(8,128)(2,1)}, u32[]{:S(2)}, u32[]{:S(2)}) %all-to-all-start.2) | async-done | bytes 12582944 | tf_op jit(solution)/shard_map/all_to_all | solution.py:31
  310.8 17.6 %copy.76 = f32[384,16384]{0,1:T(8,128)} copy(bf16[384,16384]{1,0:T(8,128)(2,1)} %param.11) | data formatting | bytes 37748736 | tf_op jit(solution)/shard_map/convert_element_type | solution.py:29
  328.4 24.6 %copy.82 = f32[384,32,512]{2,0,1:T(8,128)} copy(f32[384,32,512]{0,2,1:T(8,128)} %bitcast.80) | data formatting | bytes 50331648 | tf_op jit(solution)/shard_map/convert_element_type | solution.py:84
  353.0 14.4 %copy.77 = bf16[48,8,16384]{2,1,0:T(8,128)(2,1)} copy(bf16[48,8,16384]{2,0,1:T(8,128)(2,1)} %bitcast.12) | data formatting | bytes 25165824 | tf_op jit(solution)/shard_map/all_to_all | solution.py:31
  367.4 19.5 %reshape.53 = bf16[48,256,512]{2,1,0:T(8,128)(2,1)} reshape(bf16[48,8,16384]{2,1,0:T(8,128)(2,1)} %copy.77) | data formatting | bytes 25165824 | tf_op jit(solution)/shard_map/reshape | solution.py:38
  387.0 18.9 %fusion.1 = (f32[48,512]{1,0:T(8,128)}, f32[48,256,512]{2,1,0:T(8,128)}) fusion(bf16[48,512,256]{1,2,0:T(8,128)(2,1)} %convolution_convert_fusion, bf16[48,256,512]{2,1,0:T(8,128)(2,1)} %reshape.53, bf16[512,512]{1,0:T(8,128)(2,1)S(1)} %copy-done.3), kind=kOutput, calls=%fused_computation.3 | convolution fusion | flops 6461300736 | bytes 50954240 | tf_op jit(solution)/shard_map/cij,jk->cik/dot_general | solution.py:40
  405.9 16.3 %fusion.21 = f32[48,512,256]{2,1,0:T(8,128)} fusion(f32[48,256,512]{2,1,0:T(8,128)} %get-tuple-element.45, f32[48,512]{1,0:T(8,128)S(1)} %constant_dynamic-slice_fusion, bf16[256,256]{1,0:T(8,128)(2,1)S(1)} %copy-done.6), kind=kOutput, calls=%fused_computation.22 | convolution fusion | flops 3233808384 | bytes 50561024 | tf_op jit(solution)/shard_map/ki,cij->ckj/dot_general | solution.py:42
  422.2 14.5 %convert_bitcast_fusion = bf16[48,256,512]{1,2,0:T(8,128)(2,1)} fusion(f32[48,512,256]{2,1,0:T(8,128)} %fusion.21, f32[48,256]{1,0:T(8,128)S(1)} %constant_dynamic-slice_fusion.1, bf16[256,256]{1,0:T(8,128)(2,1)S(1)} %copy-done.7), kind=kOutput, calls=%fused_computation.14 | convolution fusion | flops 3240099840 | bytes 37928960 | tf_op jit(solution)/shard_map/ki,cij->ckj/dot_general | solution.py:44
  436.7 16.7 %copy.79 = bf16[48,256,512]{2,1,0:T(8,128)(2,1)} copy(bf16[48,256,512]{1,2,0:T(8,128)(2,1)} %convert_bitcast_fusion) | data formatting | bytes 25165824 | tf_op jit(solution)/shard_map/convert_element_type | solution.py:44
  453.4 19.5 %all_to_all.60 = bf16[48,8,16384]{2,1,0:T(8,128)(2,1)} reshape(bf16[48,256,512]{2,1,0:T(8,128)(2,1)} %copy.79) | data formatting | bytes 25165824 | tf_op jit(solution)/shard_map/all_to_all | solution.py:69
  472.9 26.0 %copy.80 = bf16[48,8,16384]{2,0,1:T(8,128)(2,1)} copy(bf16[48,8,16384]{2,1,0:T(8,128)(2,1)} %all_to_all.60) | data formatting | bytes 25165824 | tf_op jit(solution)/shard_map/all_to_all | solution.py:69
  499.0 16.0 %fusion.28 = f32[256,256]{1,0:T(8,128)} fusion(bf16[48,256,512]{2,1,0:T(8,128)(2,1)} %copy-done.2, f32[48,512,256]{2,1,0:T(8,128)} %fusion.21, f32[48,256]{1,0:T(8,128)S(1)} %constant_dynamic-slice_fusion.1), kind=kOutput, calls=%fused_computation.26 | convolution fusion | flops 3233808384 | bytes 38060032 | tf_op jit(solution)/shard_map/ckj,cij->ki/dot_general | solution.py:51
  520.3 14.1 %fusion.22 = f32[512,512]{0,1:T(8,128)} fusion(bf16[48,256,512]{2,1,0:T(8,128)(2,1)} %reshape.53, bf16[48,512,256]{1,2,0:T(8,128)(2,1)} %convolution_convert_fusion, f32[48,512]{1,0:T(8,128)S(1)} %constant_dynamic-slice_fusion), kind=kOutput, calls=%fused_computation.23 | convolution fusion | flops 6461325312 | bytes 26312704 | tf_op jit(solution)/shard_map/cij,cik->jk/dot_general | solution.py:61
  534.4 12.6 %convolution_bitcast_fusion = f32[512,512]{0,1:T(8,128)} fusion(bf16[48,256,512]{1,2,0:T(8,128)(2,1)} %convert_bitcast_fusion, bf16[48,256,512]{2,1,0:T(8,128)(2,1)} %reshape.52), kind=kOutput, calls=%fused_computation.24 | convolution fusion | flops 6442450944 | bytes 26214400 | tf_op jit(solution)/shard_map/cij,cik->jk/dot_general | solution.py:47
  547.0 17.6 %fusion.25 = f32[256,256]{1,0:T(8,128)} fusion(f32[48,256,512]{2,1,0:T(8,128)} %get-tuple-element.45, f32[48,512]{1,0:T(8,128)S(1)} %constant_dynamic-slice_fusion, f32[48,512,256]{2,1,0:T(8,128)} %fusion.39, f32[48,256]{1,0:T(8,128)S(1)} %constant_dynamic-slice_fusion.1), kind=kOutput, calls=%fused_computation.25 | convolution fusion | flops 3246391296 | bytes 50741248 | tf_op jit(solution)/shard_map/ckj,cij->ki/dot_general | solution.py:55
  564.6 16.7 %multiply_reduce_fusion = f32[48,256]{1,0:T(8,128)S(1)} fusion(f32[48,512,256]{2,1,0:T(8,128)} %fusion.39, f32[48,512,256]{2,1,0:T(8,128)} %fusion.21), kind=kLoop, calls=%fused_computation.4 | loop fusion | flops 12570624 | bytes 50380800 | tf_op jit(solution)/shard_map/reduce_sum | solution.py:53
  581.3 89.7 %all_gather.7 = f32[384,256]{1,0:T(8,128)S(1)} all-gather(f32[48,256]{1,0:T(8,128)S(1)} %multiply_reduce_fusion), channel_id=1, replica_groups=mesh['seq'=8,'ch'=4] {'seq'}, dimensions={0}, use_global_device_ids=true | all-gather | bytes 442368 | tf_op jit(solution)/shard_map/all_gather | solution.py:75
  682.0 62.6 %all-reduce.3.cloned.1.call-done = (f32[512,512]{0,1:T(8,128)}, f32[256,256]{1,0:T(8,128)}, f32[256,256]{1,0:T(8,128)}, f32[512,512]{0,1:T(8,128)}) async-done(((f32[512,512]{0,1:T(8,128)}, f32[256,256]{1,0:T(8,128)}, f32[256,256]{1,0:T(8,128)}, f32[512,512]{0,1:T(8,128)}), (f32[512,512]{0,1:T(8,128)}, f32[256,256]{1,0:T(8,128)}, f32[256,256]{1,0:T(8,128)}, ...) | async-done | bytes 2621456 | tf_op jit(solution)/shard_map/psum | solution.py:88
  750.8 12.8 %copy.101 = bf16[48,8,32,512]{3,2,1,0:T(8,128)(2,1)} copy(bf16[48,8,32,512]{3,1,2,0:T(8,128)(2,1)} %bitcast.26) | data formatting | bytes 25165824
  763.6 65.3 %multiply_convert_fusion = bf16[384,32,512]{2,0,1:T(8,128)(2,1)} fusion(f32[384,32,512]{2,0,1:T(8,128)} %copy.82, bf16[384,32,512]{2,1,0:T(8,128)(2,1)} %bitcast.81, bf16[512,512]{1,0:T(8,128)(2,1)S(1)} %copy-done.5), kind=kOutput, calls=%fused_computation.5 | convolution fusion | flops 6455033856 | bytes 50855936 | tf_op jit(solution)/shard_map/cij,jk->cik/dot_general | solution.py:77
  828.9 16.7 %copy.83 = bf16[384,32,512]{0,2,1:T(8,128)(2,1)} copy(bf16[384,32,512]{2,0,1:T(8,128)(2,1)} %multiply_convert_fusion) | data formatting | bytes 25165824 | tf_op jit(solution)/shard_map/convert_element_type | solution.py:85
  845.6 16.6 %copy.88 = bf16[384,16384]{1,0:T(8,128)(2,1)} copy(bf16[384,16384]{0,1:T(8,128)(2,1)} %bitcast.83) | data formatting | bytes 25165824
  862.2 10.5 %copy.111 = bf16[384,16384]{1,0:T(8,128)(2,1)} copy(bf16[384,16384]{1,0:T(8,128)(2,1)} %bitcast.9) | data formatting | bytes 25165824
  (35 shorter events, 48.6 us)
Async XLA Ops:
  7.2 160.1 %copy-start = (f32[384,512]{1,0:T(8,128)S(1)}, f32[384,512]{1,0:T(8,128)}, u32[]{:S(2)}) copy-start(f32[384,512]{1,0:T(8,128)} %param.16) | copy-start | bytes 2359300
  161.1 144.4 %all-to-all-start.2 = ((bf16[8,48,16384]{2,1,0:T(8,128)(2,1)}), bf16[8,48,16384]{2,1,0:T(8,128)(2,1)}, u32[]{:S(2)}, u32[]{:S(2)}) async-start(bf16[8,48,16384]{2,1,0:T(8,128)(2,1)} %bitcast.85), calls=%async_computation.2 | async-start | bytes 25165824 | tf_op jit(solution)/shard_map/all_to_all | solution.py:31
  181.7 19.5 %copy-start.4 = (bf16[512,512]{1,0:T(8,128)(2,1)S(1)}, bf16[512,512]{1,0:T(8,128)(2,1)}, u32[]{:S(2)}) copy-start(bf16[512,512]{1,0:T(8,128)(2,1)} %param.15) | copy-start | bytes 1572868
  201.3 16.1 %copy-start.7 = (bf16[256,256]{1,0:T(8,128)(2,1)S(1)}, bf16[256,256]{1,0:T(8,128)(2,1)}, u32[]{:S(2)}) copy-start(bf16[256,256]{1,0:T(8,128)(2,1)} %param.14) | copy-start | bytes 393220
  212.8 4.5 copy-start.2
  217.4 10.1 %copy-start.6 = (bf16[256,256]{1,0:T(8,128)(2,1)S(1)}, bf16[256,256]{1,0:T(8,128)(2,1)}, u32[]{:S(2)}) copy-start(bf16[256,256]{1,0:T(8,128)(2,1)} %param.13) | copy-start | bytes 393220
  227.5 14.8 %copy-start.3 = (bf16[512,512]{1,0:T(8,128)(2,1)S(1)}, bf16[512,512]{1,0:T(8,128)(2,1)}, u32[]{:S(2)}) copy-start(bf16[512,512]{1,0:T(8,128)(2,1)} %param.12) | copy-start | bytes 1572868
  305.4 209.5 %all-to-all-start.1 = ((bf16[48,8,16384]{2,0,1:T(8,128)(2,1)}), bf16[48,8,16384]{2,0,1:T(8,128)(2,1)}, u32[]{:S(2)}, u32[]{:S(2)}) async-start(bf16[48,8,16384]{2,0,1:T(8,128)(2,1)} %copy.75), calls=%async_computation.1 | async-start | bytes 25165824 | tf_op jit(solution)/shard_map/all_to_all | solution.py:66
  514.9 235.9 %all-to-all-start.3 = ((bf16[48,8,16384]{2,0,1:T(8,128)(2,1)}), bf16[48,8,16384]{2,0,1:T(8,128)(2,1)}, u32[]{:S(2)}, u32[]{:S(2)}) async-start(bf16[48,8,16384]{2,0,1:T(8,128)(2,1)} %copy.80), calls=%async_computation.3 | async-start | bytes 25165824 | tf_op jit(solution)/shard_map/all_to_all | solution.py:69
  520.3 224.3 %all-reduce.3.cloned.1.call-start = ((), (), s32[]{:S(2)}) async-start(), calls=%async_computation.4 | async-start | bytes 5242880 | tf_op jit(solution)/shard_map/psum | solution.py:88
  564.6 106.4 %copy-start.8 = (f32[48,512]{1,0:T(8,128)S(1)}, f32[48,512]{1,0:T(8,128)}, u32[]{:S(2)}) copy-start(f32[48,512]{1,0:T(8,128)} %get-tuple-element.44) | copy-start | bytes 294916
  750.8 12.8 %copy-start.5 = (bf16[512,512]{1,0:T(8,128)(2,1)S(1)}, bf16[512,512]{1,0:T(8,128)(2,1)}, u32[]{:S(2)}) copy-start(bf16[512,512]{1,0:T(8,128)(2,1)} %param.15) | copy-start | bytes 1572868
  862.2 10.5 %copy-start.1 = (f32[384,512]{1,0:T(8,128)S(1)}, f32[384,512]{1,0:T(8,128)}, u32[]{:S(2)}) copy-start(f32[384,512]{1,0:T(8,128)} %param.16) | copy-start | bytes 2359300
Sparse Core Ops, SparseCore 0:
  564.7 179.7 all-reduce.2
where the time goes:
time: 894 us; the launch traced here: 880 us
  local copies, waits for them, and re-layouts  271 us (30%)
  blocking collectives  243 us (27%)
  matrix products  226 us (25%)
  waiting for transfers between devices  77.1 us (9%)
  other arithmetic  31.9 us (4%)
  starting transfers between devices  16.1 us (2%)
  between operations  14.5 us (2%)
    all_to_all x1, blocking collectives, local(): lax.all_to_all(up_gate, 'seq', split_axis=0, concat_axis=1, tiled=True)  144 us
    all_gather x1, blocking collectives, local(): lax.all_gather(rows_part, 'seq', axis=0, tiled=True)  89.7 us
    dot_general x1, matrix products, local(): jnp.einsum('cij,jk->cik', second_rows.reshape(width, rows_local, P2), fac...  65.3 us
    psum x1, waiting for transfers between devices, local(): lax.psum((grad_one, grad_two, grad_three, grad_four), ('seq', 'ch'))  62.6 us
    unnamed x23, local copies, waits for them, and re-layouts  47.1 us
    all_to_all x2, local copies, waits for them, and re-layouts, local(): lax.all_to_all(second.reshape(several, P1 * P2), 'seq', split_axis=1, con...  45.5 us
    all_to_all x2, local copies, waits for them, and re-layouts, local(): lax.all_to_all(local_input.reshape(several, P1 * P2), 'seq', split_axis=1...  34.3 us
    convert_element_type x1, local copies, waits for them, and re-layouts, local(): upstream.reshape(width, rows_local, P2).astype(flt) * final_prod  24.6 us
  transfers between devices with their start and end apart: 4, of which 2 were waited for; matrix products, arithmetic and copies ran while one was open for 40% of the time, Pallas kernels for 0%

commit v1 on v0

--- a/solution.py
+++ b/solution.py
@@ -7,6 +7,17 @@
 P1 = 256
 P2 = 512
 C = 1536
+
+
+def collect(x, axis, dim):
+    ways = lax.axis_size(axis)
+    pieces = [x]
+    for far in range(1, ways):
+        pieces.append(
+            lax.ppermute(pieces[far - 1], axis, [(d, (d - 1) % ways) for d in range(ways)])
+        )
+    line = jnp.concatenate(pieces, axis=dim)
+    return jnp.roll(line, lax.axis_index(axis) * x.shape[dim], axis=dim)
 
 
 def local(
@@ -72,7 +83,7 @@
     )
     cols_sum, rows_sum = (
         lax.all_gather(cols_part, "seq", axis=0, tiled=True),
-        lax.all_gather(rows_part, "seq", axis=0, tiled=True),
+        collect(rows_part, "seq", 0),
     )
     final_prod = jnp.einsum(
         "cij,jk->cik",

time: 894 us -> 966 us (1.081)
  waiting for transfers between devices: 77.1 us -> 351 us
  blocking collectives: 243 us -> 26.4 us
  starting transfers between devices: 16.1 us -> 40.4 us
  local copies, waits for them, and re-layouts: 271 us -> 260 us
    all_to_all x1 -> x0, blocking collectives: 144 us -> none  [local(): lax.all_to_all(up_gate, 'seq', split_axis=0, concat_axis=1, tiled=True)]
    all_to_all x1, waiting for transfers between devices: 14.5 us -> 126 us  [local(): lax.all_to_all(inputs, 'seq', split_axis=0, concat_axis=1, tiled=True)]
    ppermute x0 -> x7, waiting for transfers between devices: none -> 105 us  [collect(): lax.ppermute(pieces[far - 1], axis, [(d, (d - 1) % ways) for d in range(w...]
    all_gather x1 -> x0, blocking collectives: 89.7 us -> none  [local(): lax.all_gather(rows_part, 'seq', axis=0, tiled=True)]
    all_to_all x0 -> x1, waiting for transfers between devices: none -> 61.9 us  [local(): lax.all_to_all(up_gate, 'seq', split_axis=0, concat_axis=1, tiled=True)]
    ppermute x0 -> x7, starting transfers between devices: none -> 18.8 us  [collect(): lax.ppermute(pieces[far - 1], axis, [(d, (d - 1) % ways) for d in range(w...]
    all_gather x1, blocking collectives: 9.24 us -> 26.4 us  [local(): lax.all_gather(cols_part, 'seq', axis=0, tiled=True)]
    all_to_all x2, local copies, waits for them, and re-layouts: 45.5 us -> 34 us  [local(): lax.all_to_all(second.reshape(several, P1 * P2), 'seq', split_axis=1, con...]
  transfers between devices with their start and end apart: 4 -> 12, of which waited for: 2 -> 9; matrix products, arithmetic and copies ran while one was open for 40% -> 27% of each run, Pallas kernels for 0% -> 0%
where the time goes in v1:
time: 966 us; the launch traced here: 952 us
  waiting for transfers between devices  351 us (36%)
  local copies, waits for them, and re-layouts  260 us (27%)
  matrix products  225 us (23%)
  starting transfers between devices  40.4 us (4%)
  other arithmetic  35.4 us (4%)
  blocking collectives  26.4 us (3%)
  between operations  14.6 us (2%)
    all_to_all x1, waiting for transfers between devices, local(): lax.all_to_all(inputs, 'seq', split_axis=0, concat_axis=1, tiled=True)  126 us
    ppermute x7, waiting for transfers between devices, collect(): lax.ppermute(pieces[far - 1], axis, [(d, (d - 1) % ways) for d in range(w...  105 us
    dot_general x1, matrix products, local(): jnp.einsum('cij,jk->cik', second_rows.reshape(width, rows_local, P2), fac...  65.3 us
    all_to_all x1, waiting for transfers between devices, local(): lax.all_to_all(up_gate, 'seq', split_axis=0, concat_axis=1, tiled=True)  61.9 us
    psum x1, waiting for transfers between devices, local(): lax.psum((grad_one, grad_two, grad_three, grad_four), ('seq', 'ch'))  58.3 us
    unnamed x36, local copies, waits for them, and re-layouts  47.1 us
    all_to_all x2, local copies, waits for them, and re-layouts, local(): lax.all_to_all(local_input.reshape(several, P1 * P2), 'seq', split_axis=1...  34 us
    all_to_all x2, local copies, waits for them, and re-layouts, local(): lax.all_to_all(second.reshape(several, P1 * P2), 'seq', split_axis=1, con...  34 us
  transfers between devices with their start and end apart: 12, of which 9 were waited for; matrix products, arithmetic and copies ran while one was open for 27% of the time, Pallas kernels for 0%

profile of v1, /device:TPU:0, one launch (start us, length us, event | category | flops | bytes accessed | tf_op | source)
XLA Modules:
  0.0 952.4 jit_solution(13539324114695081341)
XLA Ops:
  12.7 13.8 %multiply_convert_fusion.4 = bf16[384,16384]{1,0:T(8,128)(2,1)} fusion(bf16[384,16384]{1,0:T(8,128)(2,1)} %param.10, bf16[384,16384]{1,0:T(8,128)(2,1)} %param.11), kind=kLoop, calls=%fused_computation.9 | loop fusion | flops 25165824 | bytes 37748736 | tf_op jit(solution)/shard_map/convert_element_type | solution.py:40
  26.5 125.9 %all-to-all-done.2 = bf16[8,48,16384]{2,1,0:T(8,128)(2,1)} async-done(((bf16[8,48,16384]{2,1,0:T(8,128)(2,1)}), bf16[8,48,16384]{2,1,0:T(8,128)(2,1)}, u32[]{:S(2)}, u32[]{:S(2)}) %all-to-all-start.2) | async-done | bytes 12582944 | tf_op jit(solution)/shard_map/all_to_all | solution.py:42
  157.8 17.6 %copy.76 = f32[384,16384]{0,1:T(8,128)} copy(bf16[384,16384]{1,0:T(8,128)(2,1)} %param.11) | data formatting | bytes 37748736 | tf_op jit(solution)/shard_map/convert_element_type | solution.py:40
  175.4 24.7 %copy.82 = f32[384,32,512]{2,0,1:T(8,128)} copy(f32[384,32,512]{0,2,1:T(8,128)} %bitcast.80) | data formatting | bytes 50331648 | tf_op jit(solution)/shard_map/convert_element_type | solution.py:95
  200.9 14.4 %copy.77 = bf16[48,8,16384]{2,1,0:T(8,128)(2,1)} copy(bf16[48,8,16384]{2,0,1:T(8,128)(2,1)} %bitcast.12) | data formatting | bytes 25165824 | tf_op jit(solution)/shard_map/all_to_all | solution.py:42
  215.3 19.5 %reshape.53 = bf16[48,256,512]{2,1,0:T(8,128)(2,1)} reshape(bf16[48,8,16384]{2,1,0:T(8,128)(2,1)} %copy.77) | data formatting | bytes 25165824 | tf_op jit(solution)/shard_map/reshape | solution.py:49
  234.9 61.9 %all-to-all-done = bf16[8,48,16384]{2,1,0:T(8,128)(2,1)} async-done(((bf16[8,48,16384]{2,1,0:T(8,128)(2,1)}), bf16[8,48,16384]{2,1,0:T(8,128)(2,1)}, u32[]{:S(2)}, u32[]{:S(2)}) %all-to-all-start) | async-done | bytes 12582944 | tf_op jit(solution)/shard_map/all_to_all | solution.py:43
  296.7 14.4 %copy.71 = bf16[48,8,16384]{2,1,0:T(8,128)(2,1)} copy(bf16[48,8,16384]{2,0,1:T(8,128)(2,1)} %bitcast.1) | data formatting | bytes 25165824 | tf_op jit(solution)/shard_map/all_to_all | solution.py:43
  311.1 19.5 %reshape.52 = bf16[48,256,512]{2,1,0:T(8,128)(2,1)} reshape(bf16[48,8,16384]{2,1,0:T(8,128)(2,1)} %copy.71) | data formatting | bytes 25165824 | tf_op jit(solution)/shard_map/reshape | solution.py:50
  330.7 11.6 %convolution_convert_fusion.1 = bf16[48,256,512]{2,1,0:T(8,128)(2,1)S(1)} fusion(bf16[48,256,512]{2,1,0:T(8,128)(2,1)} %reshape.52, bf16[512,512]{1,0:T(8,128)(2,1)S(1)} %copy-done.4), kind=kOutput, calls=%fused_computation.19 | convolution fusion | flops 6448742400 | bytes 25690112 | tf_op jit(solution)/shard_map/cik,jk->cij/dot_general | solution.py:59
  356.8 14.8 %convolution_convert_fusion = bf16[48,512,256]{1,2,0:T(8,128)(2,1)} fusion(f32[48,512,256]{2,1,0:T(8,128)} %fusion.39, f32[48,256]{1,0:T(8,128)S(1)} %constant_dynamic-slice_fusion.1, bf16[256,256]{1,0:T(8,128)(2,1)S(1)} %copy-done.6), kind=kOutput, calls=%fused_computation.17 | convolution fusion | flops 3240099840 | bytes 37928960 | tf_op jit(solution)/shard_map/ki,ckj->cij/dot_general | solution.py:67
  371.6 14.6 %fusion.10 = bf16[48,256,512]{2,1,0:T(8,128)(2,1)} fusion(bf16[48,512,256]{1,2,0:T(8,128)(2,1)} %convolution_convert_fusion, f32[48,512]{1,0:T(8,128)S(1)} %constant_dynamic-slice_fusion, bf16[512,512]{1,0:T(8,128)(2,1)S(1)} %copy-done.3), kind=kOutput, calls=%fused_computation.18 | convolution fusion | flops 6467616768 | bytes 25788416 | tf_op jit(solution)/shard_map/cik,jk->cij/dot_general | solution.py:73
  386.2 19.5 %all_to_all.53 = bf16[48,8,16384]{2,1,0:T(8,128)(2,1)} reshape(bf16[48,256,512]{2,1,0:T(8,128)(2,1)} %fusion.10) | data formatting | bytes 25165824 | tf_op jit(solution)/shard_map/all_to_all | solution.py:77
  405.7 14.5 %copy.75 = bf16[48,8,16384]{2,0,1:T(8,128)(2,1)} copy(bf16[48,8,16384]{2,1,0:T(8,128)(2,1)} %all_to_all.53) | data formatting | bytes 25165824 | tf_op jit(solution)/shard_map/all_to_all | solution.py:77
  425.6 18.4 %fusion.1 = (f32[48,512]{1,0:T(8,128)S(1)}, f32[48,256,512]{2,1,0:T(8,128)}) fusion(bf16[48,512,256]{1,2,0:T(8,128)(2,1)} %convolution_convert_fusion, bf16[48,256,512]{2,1,0:T(8,128)(2,1)} %reshape.53, bf16[512,512]{1,0:T(8,128)(2,1)S(1)} %copy-done.3), kind=kOutput, calls=%fused_computation.3 | convolution fusion | flops 6461300736 | bytes 50954240 | tf_op jit(solution)/shard_map/cij,jk->cik/dot_general | solution.py:51
  443.9 16.2 %fusion.21 = f32[48,512,256]{2,1,0:T(8,128)} fusion(f32[48,256,512]{2,1,0:T(8,128)} %get-tuple-element.45, f32[48,512]{1,0:T(8,128)S(1)} %constant_dynamic-slice_fusion, bf16[256,256]{1,0:T(8,128)(2,1)S(1)} %copy-done.6), kind=kOutput, calls=%fused_computation.22 | convolution fusion | flops 3233808384 | bytes 50561024 | tf_op jit(solution)/shard_map/ki,cij->ckj/dot_general | solution.py:53
  460.1 14.5 %convert_bitcast_fusion = bf16[48,256,512]{1,2,0:T(8,128)(2,1)} fusion(f32[48,512,256]{2,1,0:T(8,128)} %fusion.21, f32[48,256]{1,0:T(8,128)S(1)} %constant_dynamic-slice_fusion.1, bf16[256,256]{1,0:T(8,128)(2,1)S(1)} %copy-done.7), kind=kOutput, calls=%fused_computation.14 | convolution fusion | flops 3240099840 | bytes 37928960 | tf_op jit(solution)/shard_map/ki,cij->ckj/dot_general | solution.py:55
  474.6 16.7 %copy.79 = bf16[48,256,512]{2,1,0:T(8,128)(2,1)} copy(bf16[48,256,512]{1,2,0:T(8,128)(2,1)} %convert_bitcast_fusion) | data formatting | bytes 25165824 | tf_op jit(solution)/shard_map/convert_element_type | solution.py:55
  491.3 19.6 %all_to_all.60 = bf16[48,8,16384]{2,1,0:T(8,128)(2,1)} reshape(bf16[48,256,512]{2,1,0:T(8,128)(2,1)} %copy.79) | data formatting | bytes 25165824 | tf_op jit(solution)/shard_map/all_to_all | solution.py:80
  510.8 14.5 %copy.80 = bf16[48,8,16384]{2,0,1:T(8,128)(2,1)} copy(bf16[48,8,16384]{2,1,0:T(8,128)(2,1)} %all_to_all.60) | data formatting | bytes 25165824 | tf_op jit(solution)/shard_map/all_to_all | solution.py:80
  525.3 16.2 %multiply_reduce_fusion = f32[48,256]{1,0:T(8,128)S(1)} fusion(f32[48,512,256]{2,1,0:T(8,128)} %fusion.39, f32[48,512,256]{2,1,0:T(8,128)} %fusion.21), kind=kLoop, calls=%fused_computation.4 | loop fusion | flops 12570624 | bytes 50380800 | tf_op jit(solution)/shard_map/reduce_sum | solution.py:64
  544.1 26.4 %all_gather.3 = f32[384,512]{1,0:T(8,128)S(1)} all-gather(f32[48,512]{1,0:T(8,128)S(1)} %get-tuple-element.44), channel_id=1, replica_groups=mesh['seq'=8,'ch'=4] {'seq'}, dimensions={0}, use_global_device_ids=true | all-gather | bytes 884736 | tf_op jit(solution)/shard_map/all_gather | solution.py:85
  570.4 15.9 %fusion.28 = f32[256,256]{1,0:T(8,128)} fusion(bf16[48,256,512]{2,1,0:T(8,128)(2,1)} %copy-done.2, f32[48,512,256]{2,1,0:T(8,128)} %fusion.21, f32[48,256]{1,0:T(8,128)S(1)} %constant_dynamic-slice_fusion.1), kind=kOutput, calls=%fused_computation.26 | convolution fusion | flops 3233808384 | bytes 38060032 | tf_op jit(solution)/shard_map/ckj,cij->ki/dot_general | solution.py:62
  592.7 14.1 %fusion.22 = f32[512,512]{0,1:T(8,128)} fusion(bf16[48,256,512]{2,1,0:T(8,128)(2,1)} %reshape.53, bf16[48,512,256]{1,2,0:T(8,128)(2,1)} %convolution_convert_fusion, f32[48,512]{1,0:T(8,128)S(1)} %constant_dynamic-slice_fusion), kind=kOutput, calls=%fused_computation.23 | convolution fusion | flops 6461325312 | bytes 26312704 | tf_op jit(solution)/shard_map/cij,cik->jk/dot_general | solution.py:72
  606.7 12.6 %convolution_bitcast_fusion = f32[512,512]{0,1:T(8,128)} fusion(bf16[48,256,512]{1,2,0:T(8,128)(2,1)} %convert_bitcast_fusion, bf16[48,256,512]{2,1,0:T(8,128)(2,1)} %reshape.52), kind=kOutput, calls=%fused_computation.24 | convolution fusion | flops 6442450944 | bytes 26214400 | tf_op jit(solution)/shard_map/cij,cik->jk/dot_general | solution.py:58
  619.4 17.6 %fusion.25 = f32[256,256]{1,0:T(8,128)} fusion(f32[48,256,512]{2,1,0:T(8,128)} %get-tuple-element.45, f32[48,512]{1,0:T(8,128)S(1)} %constant_dynamic-slice_fusion, f32[48,512,256]{2,1,0:T(8,128)} %fusion.39, f32[48,256]{1,0:T(8,128)S(1)} %constant_dynamic-slice_fusion.1), kind=kOutput, calls=%fused_computation.25 | convolution fusion | flops 3246391296 | bytes 50741248 | tf_op jit(solution)/shard_map/ckj,cij->ki/dot_general | solution.py:66
  639.5 95.9 %collective-permute-done.1 = f32[48,256]{1,0:T(8,128)S(1)} collective-permute-done((f32[48,256]{1,0:T(8,128)S(1)}, f32[48,256]{1,0:T(8,128)S(1)}, u32[]{:S(2)}, u32[]{:S(2)}) %collective-permute-start.1) | collective-permute-done | bytes 49184 | tf_op jit(solution)/shard_map/ppermute | solution.py:17
  758.7 58.3 %all-reduce.3.cloned.1.call-done = (f32[512,512]{0,1:T(8,128)}, f32[256,256]{1,0:T(8,128)}, f32[256,256]{1,0:T(8,128)}, f32[512,512]{0,1:T(8,128)}) async-done(((f32[512,512]{0,1:T(8,128)}, f32[256,256]{1,0:T(8,128)}, f32[256,256]{1,0:T(8,128)}, f32[512,512]{0,1:T(8,128)}), (f32[512,512]{0,1:T(8,128)}, f32[256,256]{1,0:T(8,128)}, f32[256,256]{1,0:T(8,128)}, ...) | async-done | bytes 2621456 | tf_op jit(solution)/shard_map/psum | solution.py:99
  823.3 12.8 %copy.101 = bf16[48,8,32,512]{3,2,1,0:T(8,128)(2,1)} copy(bf16[48,8,32,512]{3,1,2,0:T(8,128)(2,1)} %bitcast.26) | data formatting | bytes 25165824
  836.1 65.3 %multiply_convert_fusion = bf16[384,32,512]{2,0,1:T(8,128)(2,1)} fusion(f32[384,32,512]{2,0,1:T(8,128)} %copy.82, bf16[384,32,512]{2,1,0:T(8,128)(2,1)} %bitcast.81, bf16[512,512]{1,0:T(8,128)(2,1)S(1)} %copy-done.5), kind=kOutput, calls=%fused_computation.5 | convolution fusion | flops 6455033856 | bytes 50855936 | tf_op jit(solution)/shard_map/cij,jk->cik/dot_general | solution.py:88
  901.4 16.6 %copy.83 = bf16[384,32,512]{0,2,1:T(8,128)(2,1)} copy(bf16[384,32,512]{2,0,1:T(8,128)(2,1)} %multiply_convert_fusion) | data formatting | bytes 25165824 | tf_op jit(solution)/shard_map/convert_element_type | solution.py:96
  918.0 16.6 %copy.88 = bf16[384,16384]{1,0:T(8,128)(2,1)} copy(bf16[384,16384]{0,1:T(8,128)(2,1)} %bitcast.82) | data formatting | bytes 25165824
  (63 shorter events, 83.1 us)
Async XLA Ops:
  7.2 193.7 %copy-start = (f32[384,512]{1,0:T(8,128)S(1)}, f32[384,512]{1,0:T(8,128)}, u32[]{:S(2)}) copy-start(f32[384,512]{1,0:T(8,128)} %param.16) | copy-start | bytes 2359300
  7.2 145.2 %all-to-all-start.2 = ((bf16[8,48,16384]{2,1,0:T(8,128)(2,1)}), bf16[8,48,16384]{2,1,0:T(8,128)(2,1)}, u32[]{:S(2)}, u32[]{:S(2)}) async-start(bf16[8,48,16384]{2,1,0:T(8,128)(2,1)} %bitcast.84), calls=%async_computation.2 | async-start | bytes 25165824 | tf_op jit(solution)/shard_map/all_to_all | solution.py:42
  152.4 144.3 %all-to-all-start = ((bf16[8,48,16384]{2,1,0:T(8,128)(2,1)}), bf16[8,48,16384]{2,1,0:T(8,128)(2,1)}, u32[]{:S(2)}, u32[]{:S(2)}) async-start(bf16[8,48,16384]{2,1,0:T(8,128)(2,1)} %bitcast.83), calls=%async_computation | async-start | bytes 25165824 | tf_op jit(solution)/shard_map/all_to_all | solution.py:43
  311.1 19.5 %copy-start.4 = (bf16[512,512]{1,0:T(8,128)(2,1)S(1)}, bf16[512,512]{1,0:T(8,128)(2,1)}, u32[]{:S(2)}) copy-start(bf16[512,512]{1,0:T(8,128)(2,1)} %param.15) | copy-start | bytes 1572868
  330.7 16.1 %copy-start.7 = (bf16[256,256]{1,0:T(8,128)(2,1)S(1)}, bf16[256,256]{1,0:T(8,128)(2,1)}, u32[]{:S(2)}) copy-start(bf16[256,256]{1,0:T(8,128)(2,1)} %param.14) | copy-start | bytes 393220
  342.3 4.5 copy-start.2
  346.7 10.1 %copy-start.6 = (bf16[256,256]{1,0:T(8,128)(2,1)S(1)}, bf16[256,256]{1,0:T(8,128)(2,1)}, u32[]{:S(2)}) copy-start(bf16[256,256]{1,0:T(8,128)(2,1)} %param.13) | copy-start | bytes 393220
  356.8 14.8 %copy-start.3 = (bf16[512,512]{1,0:T(8,128)(2,1)S(1)}, bf16[512,512]{1,0:T(8,128)(2,1)}, u32[]{:S(2)}) copy-start(bf16[512,512]{1,0:T(8,128)(2,1)} %param.12) | copy-start | bytes 1572868
  420.2 166.1 %all-to-all-start.1 = ((bf16[48,8,16384]{2,0,1:T(8,128)(2,1)}), bf16[48,8,16384]{2,0,1:T(8,128)(2,1)}, u32[]{:S(2)}, u32[]{:S(2)}) async-start(bf16[48,8,16384]{2,0,1:T(8,128)(2,1)} %copy.75), calls=%async_computation.1 | async-start | bytes 25165824 | tf_op jit(solution)/shard_map/all_to_all | solution.py:77
  541.5 95.5 %collective-permute-start = (f32[48,256]{1,0:T(8,128)S(1)}, f32[48,256]{1,0:T(8,128)S(1)}, u32[]{:S(2)}, u32[]{:S(2)}) collective-permute-start(f32[48,256]{1,0:T(8,128)S(1)} %multiply_reduce_fusion), channel_id=1, source_target_pairs={{0,28},{4,0},{8,4},{12,8},{16,12},{20,16},{24,20},{28,24},{1,29},{... | collective-permute-start | bytes 147464 | tf_op jit(solution)/shard_map/ppermute | solution.py:17
  586.3 237.0 %all-to-all-start.3 = ((bf16[48,8,16384]{2,0,1:T(8,128)(2,1)}), bf16[48,8,16384]{2,0,1:T(8,128)(2,1)}, u32[]{:S(2)}, u32[]{:S(2)}) async-start(bf16[48,8,16384]{2,0,1:T(8,128)(2,1)} %copy.80), calls=%async_computation.3 | async-start | bytes 25165824 | tf_op jit(solution)/shard_map/all_to_all | solution.py:80
  591.7 225.4 %all-reduce.3.cloned.1.call-start = ((), (), s32[]{:S(2)}) async-start(), calls=%async_computation.4 | async-start | bytes 5242880 | tf_op jit(solution)/shard_map/psum | solution.py:99
  637.0 98.5 %collective-permute-start.1 = (f32[48,256]{1,0:T(8,128)S(1)}, f32[48,256]{1,0:T(8,128)S(1)}, u32[]{:S(2)}, u32[]{:S(2)}) collective-permute-start(f32[48,256]{1,0:T(8,128)S(1)} %collective-permute-done), channel_id=1, source_target_pairs={{0,28},{4,0},{8,4},{12,8},{16,12},{20,16},{24,20},{28,24},{1,29},{... | collective-permute-start | bytes 147464 | tf_op jit(solution)/shard_map/ppermute | solution.py:17
  735.4 4.7 collective-permute-start.2
  740.1 4.4 collective-permute-start.3
  744.5 4.4 collective-permute-start.4
  748.9 4.4 collective-permute-start.5
  753.3 4.5 collective-permute-start.6
  823.3 12.8 %copy-start.5 = (bf16[512,512]{1,0:T(8,128)(2,1)S(1)}, bf16[512,512]{1,0:T(8,128)(2,1)}, u32[]{:S(2)}) copy-start(bf16[512,512]{1,0:T(8,128)(2,1)} %param.15) | copy-start | bytes 1572868
  934.6 10.5 %copy-start.1 = (f32[384,512]{1,0:T(8,128)S(1)}, f32[384,512]{1,0:T(8,128)}, u32[]{:S(2)}) copy-start(f32[384,512]{1,0:T(8,128)} %param.16) | copy-start | bytes 2359300
Sparse Core Ops, SparseCore 0:
  637.1 179.8 all-reduce.2
